TPU v7x, 32 devices: a whole 2x2x4 slice. The times are simulated.
32 devices in a mesh: dp: 8 (over y, x, core), tensor: 4 (over z).
Axes of the slice: x: 2, y: 2, z: 4, core: 2. Of those that a mesh axis runs over, the one named last changes fastest.
Arguments:
- activations: bfloat16 [8192, 1024], P(('dp', 'tensor')), may hold values from -6 to 6
- segments: int32 [8192], P('dp'), may hold values from 0 to 31, as said below
- attn_weight: bfloat16 [1, 3, 1024, 1024], P(None, None, 'dp', 'tensor'), may hold values from -0.1875 to 0.1875
- out_weight: bfloat16 [1, 1024, 1024], P(None, 'tensor', 'dp'), may hold values from -0.75 to 0.75
- up_weight: bfloat16 [1, 1024, 4096], P(None, 'dp', 'tensor'), may hold values from -0.1875 to 0.1875
- down_weight: bfloat16 [1, 4096, 1024], P(None, 'tensor', 'dp'), may hold values from -0.09375 to 0.09375
- norm_gains: bfloat16 [1, 2, 1024], P(None, None, 'dp'), may hold values from 0.5 to 1.5
- bias_rows: bfloat16 [1, 10, 1024], P(None, None, 'dp'), may hold values from -1 to 1
- cotangent: float32 [8192, 1024], P(('dp', 'tensor')), may hold values from -6 to 6
Outputs:
- layer_output: float32 [8192, 1024], P(('dp', 'tensor'))
- input_grad: float32 [8192, 1024], P(('dp', 'tensor'))
- attn_weight_grad: float32 [1, 3, 1024, 1024], P(None, None, 'dp', 'tensor')
- out_weight_grad: float32 [1, 1024, 1024], P(None, 'tensor', 'dp')
- up_weight_grad: float32 [1, 1024, 4096], P(None, 'dp', 'tensor')
- down_weight_grad: float32 [1, 4096, 1024], P(None, 'tensor', 'dp')
- gain_grad: float32 [1, 2, 1024], P(None, None, 'dp')
- bias_grad: float32 [1, 10, 1024], P(None, None, 'dp')
Inputs may be any that keep to these rules, and one draw needn't show every extreme that they name: `segments`: within each sequence of 1024 tokens ids never fall; every document has 200 tokens or more; sequences share no id; the last document of sequence j has id 4 j + 3 and ids of sequence j lie in 4 j to 4 j + 3.
All inputs are finite; a program needn't handle non-finite values.
Results may differ from a plain program's by a relative error of at most 0.018.
Values may be sent and summed in bfloat16 or wider, within the bound.
A program may use at most 128 MiB of HBM per device.

v0:
```python
import jax
import jax.numpy as jnp
from jax import lax
from jax.sharding import PartitionSpec as P

HD = 64
SEQ = 1024
EPSILON = 1e-05
MASKED = -1e30


def layer_norm(values, gain_row, shift_row):
    center = values - jnp.mean(values, axis=-1, keepdims=True)
    spread = jnp.mean(center * center, axis=-1, keepdims=True)
    return center * lax.rsqrt(spread + EPSILON) * gain_row + shift_row


def gelu_tanh(values):
    return jax.nn.gelu(values, approximate=True)


def visible_mask(segments, first_row, seq_start, block_rows):
    query_pos = first_row + jnp.arange(block_rows)
    key_pos = seq_start + jnp.arange(SEQ)
    query_seg = lax.dynamic_slice_in_dim(segments, first_row, block_rows, 0)
    return (key_pos[None, :] <= query_pos[:, None]) & (query_seg[:, None] == segments[None, :])


def block_scores(project, segments, first_row, block_rows):
    head_count = project.shape[2] // HD
    seq_start = first_row // SEQ * SEQ
    query_rows = lax.dynamic_slice_in_dim(project, first_row, block_rows, 0)[:, 0].reshape(
        block_rows, head_count, HD
    )
    key_vecs = project[:, 1].reshape(SEQ, head_count, HD)
    value_vecs = project[:, 2].reshape(SEQ, head_count, HD)
    scores = jnp.einsum(
        "qhd,khd->hqk", query_rows, key_vecs, preferred_element_type=jnp.float32
    ) * HD ** (-0.5)
    visible = visible_mask(segments, first_row, seq_start, block_rows)
    scores = jnp.where(visible[None], scores, MASKED)
    return (query_rows, key_vecs, value_vecs, scores)


def attend(project, segments):
    token_count = project.shape[0]
    block_rows = min(512, SEQ)

    def attend_one_block(block_index):
        first_row = block_index * block_rows
        query_rows, key_vecs, value_vecs, scores = block_scores(
            project, segments, first_row, block_rows
        )
        row_max = jnp.max(scores, axis=-1, keepdims=True)
        raised = jnp.exp(scores - row_max)
        row_total = jnp.sum(raised, axis=-1, keepdims=True)
        prob_rows = (raised / row_total).astype(jnp.bfloat16)
        attended = jnp.einsum(
            "hqk,khd->qhd", prob_rows, value_vecs, preferred_element_type=jnp.float32
        )
        return (
            attended.reshape(block_rows, -1).astype(jnp.bfloat16),
            (row_max + jnp.log(row_total))[:, :, 0],
        )

    attended, log_total = lax.map(attend_one_block, jnp.arange(token_count // block_rows))
    return (attended.reshape(token_count, -1), log_total)


def attend_back(project, segments, log_total, attended_grad):
    token_count = project.shape[0]
    head_width = project.shape[2]
    head_count = head_width // HD
    block_rows = min(512, SEQ)
    per_seq = SEQ // block_rows
    factor = HD ** (-0.5)

    def one_sequence(seq_index):

        def one_one_block(totals, local_index):
            key_total, value_total = totals
            block_index = seq_index * per_seq + local_index
            first_row = block_index * block_rows
            query_rows, key_vecs, value_vecs, scores = block_scores(
                project, segments, first_row, block_rows
            )
            prob_rows = jnp.exp(scores - log_total[block_index][:, :, None])
            grad_rows = lax.dynamic_slice_in_dim(attended_grad, first_row, block_rows, 0).reshape(
                block_rows, head_count, HD
            )
            prob_grad = jnp.einsum(
                "qhd,khd->hqk", grad_rows, value_vecs, preferred_element_type=jnp.float32
            )
            inner_sum = jnp.sum(prob_rows * prob_grad, axis=-1, keepdims=True)
            score_grad = (prob_rows * (prob_grad - inner_sum)).astype(jnp.bfloat16)
            query_grad = (
                jnp.einsum("hqk,khd->qhd", score_grad, key_vecs, preferred_element_type=jnp.float32)
                * factor
            )
            key_total = (
                key_total
                + jnp.einsum(
                    "hqk,qhd->khd", score_grad, query_rows, preferred_element_type=jnp.float32
                )
                * factor
            )
            value_total = value_total + jnp.einsum(
                "hqk,qhd->khd",
                prob_rows.astype(jnp.bfloat16),
                grad_rows,
                preferred_element_type=jnp.float32,
            )
            return ((key_total, value_total), query_grad)

        start_totals = (
            jnp.zeros((SEQ, head_count, HD), jnp.float32),
            jnp.zeros((SEQ, head_count, HD), jnp.float32),
        )
        (key_total, value_total), query_grads = lax.scan(
            one_one_block, start_totals, jnp.arange(per_seq)
        )
        return (
            query_grads.reshape(SEQ, head_width),
            key_total.reshape(SEQ, head_width),
            value_total.reshape(SEQ, head_width),
        )

    query_grads, key_grads, value_grads = lax.map(one_sequence, jnp.arange(token_count // SEQ))
    stacked = jnp.stack(
        [
            query_grads.reshape(token_count, head_width),
            key_grads.reshape(token_count, head_width),
            value_grads.reshape(token_count, head_width),
        ],
        axis=1,
    )
    return stacked.astype(jnp.bfloat16)


def fold_rows(weight, saved_act, shard_piece):
    product = lax.dot_general(
        shard_piece, weight, (((1,), (1,)), ((), ())), preferred_element_type=jnp.float32
    )
    weight_total = lax.dot_general(
        saved_act, shard_piece, (((0,), (0,)), ((), ())), preferred_element_type=jnp.float32
    )
    return (product, weight_total)


def layer_forward(residual, weights, segments, tensor_rank):
    attn_w, out_w, up_w, down_w, gain_rows, bias_rows = weights
    gain_rows = gain_rows.astype(jnp.float32)
    bias_rows = bias_rows.astype(jnp.float32)
    local_rows = residual.shape[0]
    normed = layer_norm(residual, gain_rows[0], bias_rows[0]).astype(jnp.bfloat16)
    normed_full = lax.all_gather(normed, "tensor", axis=0, tiled=True)
    head_width = attn_w.shape[2]
    column = tensor_rank * head_width
    query_bias = lax.dynamic_slice_in_dim(bias_rows[1], column, head_width, 0)
    value_bias = lax.dynamic_slice_in_dim(bias_rows[2], column, head_width, 0)
    bias_three = jnp.stack([query_bias, jnp.zeros_like(query_bias), value_bias])
    project = (
        jnp.einsum("td,cde->tce", normed_full, attn_w, preferred_element_type=jnp.float32)
        + bias_three[None]
    ).astype(jnp.bfloat16)
    attended, log_total = attend(project, segments)

    def attn_term(first_row, row_count):
        return jnp.dot(attended, out_w, preferred_element_type=jnp.float32)

    middle = residual + (
        lax.psum_scatter(
            attn_term(jnp.int32(0), local_rows * lax.axis_size("tensor")),
            "tensor",
            scatter_dimension=0,
            tiled=True,
        )
        + bias_rows[3]
    )
    normed_two = layer_norm(middle, gain_rows[1], bias_rows[4]).astype(jnp.bfloat16)
    normed_two_kept = lax.all_gather(normed_two, "tensor", axis=0, tiled=True)
    unit_width = up_w.shape[1]
    up_bias = lax.dynamic_slice_in_dim(
        bias_rows[6:10].reshape(-1), tensor_rank * unit_width, unit_width, 0
    )
    hidden = jnp.dot(normed_two_kept, up_w, preferred_element_type=jnp.float32) + up_bias
    active = gelu_tanh(hidden).astype(jnp.bfloat16)
    output = middle + (
        lax.psum_scatter(
            jnp.dot(active, down_w, preferred_element_type=jnp.float32).astype(jnp.bfloat16),
            "tensor",
            scatter_dimension=0,
            tiled=True,
        ).astype(jnp.float32)
        + bias_rows[5]
    )
    return (
        output,
        (
            residual,
            middle,
            normed_full,
            project,
            attended,
            log_total,
            normed_two_kept,
            hidden,
            active,
        ),
    )


def layer_backward(upstream, weights, stored, segments, tensor_rank):
    attn_w, out_w, up_w, down_w, gain_rows, bias_rows = weights
    gain_rows = gain_rows.astype(jnp.float32)
    bias_rows = bias_rows.astype(jnp.float32)
    residual, middle, normed_full, project, attended, log_total, normed_two_kept, hidden, active = (
        stored
    )
    local_rows = upstream.shape[0]
    model_width = residual.shape[1]
    unit_width = up_w.shape[1]
    head_width = attn_w.shape[2]
    column = tensor_rank * head_width
    branch_grad = upstream.astype(jnp.bfloat16)
    down_bias_grad = jnp.sum(branch_grad.astype(jnp.float32), axis=0)
    active_grad, down_grad = fold_rows(
        down_w, active, lax.all_gather(branch_grad, "tensor", axis=0, tiled=True)
    )
    hidden_grad = jax.vjp(gelu_tanh, hidden)[1](active_grad)[0].astype(jnp.bfloat16)
    up_bias_grad = jnp.sum(hidden_grad.astype(jnp.float32), axis=0)
    up_rows_grad = lax.dynamic_update_slice_in_dim(
        jnp.zeros((4 * model_width,), jnp.float32), up_bias_grad, tensor_rank * unit_width, 0
    ).reshape(4, model_width)
    up_grad = lax.dot_general(
        normed_two_kept, hidden_grad, (((0,), (0,)), ((), ())), preferred_element_type=jnp.float32
    )
    normed_two_grad = lax.psum_scatter(
        lax.dot_general(
            hidden_grad, up_w, (((1,), (1,)), ((), ())), preferred_element_type=jnp.float32
        ),
        "tensor",
        scatter_dimension=0,
        tiled=True,
    )
    primal, pullback = jax.vjp(layer_norm, middle, gain_rows[1], bias_rows[4])
    middle_part, gain_two_grad, shift_two_grad = pullback(normed_two_grad)
    middle_grad = upstream + middle_part
    attn_branch = middle_grad.astype(jnp.bfloat16)
    out_bias_grad = jnp.sum(attn_branch.astype(jnp.float32), axis=0)
    attended_grad, out_grad = fold_rows(
        out_w, attended, lax.all_gather(attn_branch, "tensor", axis=0, tiled=True)
    )
    project_grad = attend_back(project, segments, log_total, attended_grad.astype(jnp.bfloat16))
    query_bias_grad = jnp.sum(project_grad[:, 0].astype(jnp.float32), axis=0)
    value_bias_grad = jnp.sum(project_grad[:, 2].astype(jnp.float32), axis=0)
    attn_grad = jnp.einsum(
        "td,tce->cde", normed_full, project_grad, preferred_element_type=jnp.float32
    )

    def attn_term(first_row, row_count):
        return jnp.einsum("tce,cde->td", project_grad, attn_w, preferred_element_type=jnp.float32)

    normed_grad = lax.psum_scatter(
        attn_term(jnp.int32(0), local_rows * lax.axis_size("tensor")).astype(jnp.bfloat16),
        "tensor",
        scatter_dimension=0,
        tiled=True,
    ).astype(jnp.float32)
    primal, pullback = jax.vjp(layer_norm, residual, gain_rows[0], bias_rows[0])
    residual_part, gain_one_grad, shift_one_grad = pullback(normed_grad)
    input_grad = middle_grad + residual_part
    query_full = lax.dynamic_update_slice_in_dim(
        jnp.zeros((model_width,), jnp.float32), query_bias_grad, column, 0
    )
    value_full = lax.dynamic_update_slice_in_dim(
        jnp.zeros((model_width,), jnp.float32), value_bias_grad, column, 0
    )
    gain_grad = jnp.stack([gain_one_grad, gain_two_grad])
    bias_grad = jnp.concatenate(
        [
            jnp.stack(
                [
                    shift_one_grad,
                    query_full,
                    value_full,
                    out_bias_grad,
                    shift_two_grad,
                    down_bias_grad,
                ]
            ),
            up_rows_grad,
        ],
        axis=0,
    )
    return (input_grad, (attn_grad, out_grad, up_grad, down_grad, gain_grad, bias_grad))


def per_device(
    activations,
    segments,
    attn_weight,
    out_weight,
    up_weight,
    down_weight,
    norm_gains,
    bias_rows,
    cotangent,
):
    tensor_rank = lax.axis_index("tensor")
    layers = attn_weight.shape[0]
    residual = activations.astype(jnp.float32)
    layer_index = 0
    weights = (
        lax.all_gather(attn_weight[layer_index], "dp", axis=1, tiled=True),
        lax.all_gather(out_weight[layer_index], "dp", axis=1, tiled=True),
        lax.all_gather(up_weight[layer_index], "dp", axis=0, tiled=True),
        lax.all_gather(down_weight[layer_index], "dp", axis=1, tiled=True),
        lax.all_gather(norm_gains[layer_index], "dp", axis=1, tiled=True),
        lax.all_gather(bias_rows[layer_index], "dp", axis=1, tiled=True),
    )
    residual, saved_now = layer_forward(residual, weights, segments, tensor_rank)
    stored = [saved_now]
    upstream = cotangent
    layer_grads = [None] * layers
    for layer_index in reversed(range(layers)):
        weights = (
            lax.all_gather(attn_weight[layer_index], "dp", axis=1, tiled=True),
            lax.all_gather(out_weight[layer_index], "dp", axis=1, tiled=True),
            lax.all_gather(up_weight[layer_index], "dp", axis=0, tiled=True),
            lax.all_gather(down_weight[layer_index], "dp", axis=1, tiled=True),
            lax.all_gather(norm_gains[layer_index], "dp", axis=1, tiled=True),
            lax.all_gather(bias_rows[layer_index], "dp", axis=1, tiled=True),
        )
        upstream, grads_now = layer_backward(
            upstream, weights, stored[layer_index], segments, tensor_rank
        )
        grads_now = (
            lax.psum_scatter(
                grads_now[0].astype(jnp.bfloat16), "dp", scatter_dimension=1, tiled=True
            ).astype(jnp.float32),
            lax.psum_scatter(
                grads_now[1].astype(jnp.bfloat16), "dp", scatter_dimension=1, tiled=True
            ).astype(jnp.float32),
            lax.psum_scatter(
                grads_now[2].astype(jnp.bfloat16), "dp", scatter_dimension=0, tiled=True
            ).astype(jnp.float32),
            lax.psum_scatter(
                grads_now[3].astype(jnp.bfloat16), "dp", scatter_dimension=1, tiled=True
            ).astype(jnp.float32),
            lax.psum_scatter(
                grads_now[4].astype(jnp.bfloat16), "dp", scatter_dimension=1, tiled=True
            ).astype(jnp.float32),
            lax.psum_scatter(
                grads_now[5].astype(jnp.bfloat16), "dp", scatter_dimension=1, tiled=True
            ).astype(jnp.float32),
        )
        layer_grads[layer_index] = grads_now
    stacked = tuple(
        (jnp.stack([layer_set[member] for layer_set in layer_grads]) for member in range(6))
    )
    small_sums = lax.psum((stacked[4], stacked[5]), "tensor")
    return (
        residual,
        upstream,
        stacked[0],
        stacked[1],
        stacked[2],
        stacked[3],
        small_sums[0],
        small_sums[1],
    )


def solution(mesh):
    return jax.shard_map(
        per_device,
        mesh=mesh,
        in_specs=(
            P(("dp", "tensor"), None),
            P("dp"),
            P(None, None, "dp", "tensor"),
            P(None, "tensor", "dp"),
            P(None, "dp", "tensor"),
            P(None, "tensor", "dp"),
            P(None, None, "dp"),
            P(None, None, "dp"),
            P(("dp", "tensor"), None),
        ),
        out_specs=(
            P(("dp", "tensor"), None),
            P(("dp", "tensor"), None),
            P(None, None, "dp", "tensor"),
            P(None, "tensor", "dp"),
            P(None, "dp", "tensor"),
            P(None, "tensor", "dp"),
            P(None, None, "dp"),
            P(None, None, "dp"),
        ),
        check_vma=False,
    )
```

profile of v0, /device:TPU:0, one launch (start us, length us, event | category | flops | bytes accessed | tf_op | source)
XLA Modules:
  0.0 839.6 jit_solution(1976598825178693592)
XLA Ops:
  7.9 10.3 %all-gather = bf16[1,2,1024]{2,1,0:T(2,128)(2,1)S(1)} all-gather(bf16[1,2,128]{2,1,0:T(2,128)(2,1)} %param.19), channel_id=2, replica_groups=mesh['dp'=8,'tensor'=4] {'dp'}, dimensions={2}, use_global_device_ids=true | all-gather | bytes 4608 | tf_op jit(solution)/shard_map/all_gather | solution.py:319
  18.3 8.7 %all-gather.1 = bf16[1,10,1024]{2,1,0:T(8,128)(2,1)S(1)} all-gather(bf16[1,10,128]{2,1,0:T(8,128)(2,1)} %param.20), channel_id=3, replica_groups=mesh['dp'=8,'tensor'=4] {'dp'}, dimensions={2}, use_global_device_ids=true | all-gather | bytes 23040 | tf_op jit(solution)/shard_map/all_gather | solution.py:320
  32.5 9.9 %all-gather.3 = bf16[1,256,1024]{2,1,0:T(8,128)(2,1)S(1)} all-gather(bf16[1,256,128]{2,1,0:T(8,128)(2,1)} %param.16), channel_id=5, replica_groups=mesh['dp'=8,'tensor'=4] {'dp'}, dimensions={2}, use_global_device_ids=true | all-gather | bytes 589824 | tf_op jit(solution)/shard_map/all_gather | solution.py:316
  42.4 44.5 %all-gather.14.cloned.1.call-done = bf16[1024,1024]{1,0:T(8,128)(2,1)} async-done(((bf16[256,1024]{1,0:T(8,128)(2,1)}), bf16[1024,1024]{1,0:T(8,128)(2,1)}) %all-gather.14.cloned.1.call-update) | async-done | bytes 2097168 | tf_op jit(solution)/shard_map/all_gather | solution.py:156
  93.6 18.3 %while.43 = (s32[]{:T(128)}, bf16[2,512,256]{2,1,0:T(8,128)(2,1)S(1)}, f32[2,4,512]{2,1,0:T(4,128)S(1)}, s32[2]{0:T(128)S(1)}, s32[1024]{0:T(1024)S(1)}, /*index...) while((s32[]{:T(128)}, ...), condition=%wide.region_5.6_spmd, body=%wide.region_2.5_spmd.sunk | while | flops 563740160 | bytes 32594288 | solution.py:66
  115.2 75.0 %reduce-scatter.21.cloned.1.call-done = f32[256,1024]{1,0:T(8,128)} async-done(((f32[1024,1024]{1,0:T(8,128)}), f32[256,1024]{1,0:T(8,128)}) %reduce-scatter.21.cloned.1.call-update) | async-done | bytes 1048592 | tf_op jit(solution)/shard_map/reduce_scatter | solution.py:172
  196.8 23.8 %all-gather.24.cloned.1.call-done = bf16[1,1024,1024]{2,1,0:T(8,128)(2,1)} async-done(((bf16[1,128,1024]{2,1,0:T(8,128)(2,1)}), bf16[1,1024,1024]{2,1,0:T(8,128)(2,1)}) %all-gather.24.cloned.1.call-update) | async-done | bytes 2097168 | tf_op jit(solution)/shard_map/all_gather | solution.py:317
  220.6 48.0 %all-gather.16.cloned.1.call-done = bf16[1024,1024]{1,0:T(8,128)(2,1)} async-done(((bf16[256,1024]{1,0:T(8,128)(2,1)}), bf16[1024,1024]{1,0:T(8,128)(2,1)}) %all-gather.16.cloned.1.call-update) | async-done | bytes 2097168 | tf_op jit(solution)/shard_map/all_gather | solution.py:181
  275.1 40.3 %all-gather.18.cloned.1.call-done = bf16[1024,1024]{1,0:T(8,128)(2,1)} async-done(((bf16[256,1024]{1,0:T(8,128)(2,1)}), bf16[1024,1024]{1,0:T(8,128)(2,1)}) %all-gather.18.cloned.1.call-update) | async-done | bytes 2097168 | tf_op jit(solution)/shard_map/all_gather | solution.py:228
  315.4 29.0 %all-gather.26.cloned.1.call-done = bf16[1,1024,1024]{2,1,0:T(8,128)(2,1)} async-done(((bf16[1,1024,128]{2,1,0:T(8,128)(2,1)}), bf16[1,1024,1024]{2,1,0:T(8,128)(2,1)}) %all-gather.26.cloned.1.call-update) | async-done | bytes 2097168 | tf_op jit(solution)/shard_map/all_gather | solution.py:318
  344.4 9.0 %convert_reduce_fusion = (bf16[1024]{0:T(1024)(128)(2,1)}, bf16[1024,1024]{1,0:T(8,128)(2,1)S(1)}) fusion(f32[1024,1024]{1,0:T(8,128)} %fusion.37, f32[1024]{0:T(1024)S(1)} %dynamic_slice.68, bf16[1024,1024]{1,0:T(8,128)(2,1)} %all-gather.18.cloned.1.call-done, bf16[1,1024,1024]{2,1,0:T(8,128)(2,1)} %all-gather.26.cloned.1.call-done), kind=kOutput, calls=%fused_computation.47 | convolution fusion | flops 2171599872 | bytes 10491904 | tf_op jit(solution)/shard_map/dot_general | solution.py:141
  359.1 7.0 fusion.43
  366.1 69.8 %reduce-scatter.25.cloned.1.call-done = f32[256,1024]{1,0:T(8,128)} async-done(((f32[1024,1024]{1,0:T(8,128)}), f32[256,1024]{1,0:T(8,128)}) %reduce-scatter.25.cloned.1.call-update) | async-done | bytes 1048592 | tf_op jit(solution)/shard_map/reduce_scatter | solution.py:238
  437.5 45.1 %reduce-scatter.23.cloned.1.call-done = bf16[256,1024]{1,0:T(8,128)(2,1)} async-done(((bf16[1024,1024]{1,0:T(8,128)(2,1)}), bf16[256,1024]{1,0:T(8,128)(2,1)}) %reduce-scatter.23.cloned.1.call-update) | async-done | bytes 524304 | tf_op jit(solution)/shard_map/reduce_scatter | solution.py:189
  487.1 7.2 convolution_convert_fusion
  504.5 27.6 %all-gather.20.cloned.1.call-done = bf16[1024,1024]{1,0:T(8,128)(2,1)} async-done(((bf16[256,1024]{1,0:T(8,128)(2,1)}), bf16[1024,1024]{1,0:T(8,128)(2,1)}) %all-gather.20.cloned.1.call-update) | async-done | bytes 2097168 | tf_op jit(solution)/shard_map/all_gather | solution.py:252
  540.5 34.0 %while.44 = (s32[]{:T(128)}, f32[1024,4,64]{0,2,1:T(8,128)S(1)}, f32[1024,4,64]{0,2,1:T(8,128)}, bf16[2,512,4,64]{1,3,2,0:T(8,128)(2,1)}, s32[2]{0:T(128)S(1)}, ...) while((s32[]{:T(128)}, f32[1024,4,64]{0,2,1:T(8,128)S(1)}, ...), condition=%wide.region_15.16_spmd.clone, body=%wide.region_13.15_spmd.clone.sunk | while | flops 1376648704 | bytes 88685112 | solution.py:119
  598.6 21.5 %reduce-scatter.29.cloned.1.call-done = bf16[128,1024]{1,0:T(8,128)(2,1)} async-done(((bf16[1024,1024]{1,0:T(8,128)(2,1)}), bf16[128,1024]{1,0:T(8,128)(2,1)}) %reduce-scatter.29.cloned.1.call-update) | async-done | bytes 262160 | tf_op jit(solution)/shard_map/reduce_scatter | solution.py:345
  623.2 34.3 %reduce-scatter.33.cloned.1.call-done = bf16[128,256]{1,0:T(8,128)(2,1)} async-done(((bf16[1024,256]{1,0:T(8,128)(2,1)}), bf16[128,256]{1,0:T(8,128)(2,1)}) %reduce-scatter.33.cloned.1.call-update) | async-done | bytes 65552
  659.2 40.0 %reduce-scatter.31.cloned.1.call-done = bf16[128,768]{1,0:T(8,128)(2,1)} async-done(((bf16[1024,768]{1,0:T(8,128)(2,1)}), bf16[128,768]{1,0:T(8,128)(2,1)}) %reduce-scatter.31.cloned.1.call-update) | async-done | bytes 196624
  701.4 43.8 %reduce-scatter.27.cloned.1.call-done = bf16[256,1024]{1,0:T(8,128)(2,1)} async-done(((bf16[1024,1024]{1,0:T(8,128)(2,1)}), bf16[256,1024]{1,0:T(8,128)(2,1)}) %reduce-scatter.27.cloned.1.call-update) | async-done | bytes 524304 | tf_op jit(solution)/shard_map/reduce_scatter | solution.py:264
  753.1 29.3 %reduce-scatter.37.cloned.1.call-done = bf16[128,2]{1,0:T(8,128)(2,1)} async-done(((bf16[1024,2]{1,0:T(8,128)(2,1)}), bf16[128,2]{1,0:T(8,128)(2,1)}) %reduce-scatter.37.cloned.1.call-update) | async-done | bytes 528
  783.2 35.7 %reduce-scatter.39.cloned.1.call-done = bf16[128,10]{1,0:T(8,128)(2,1)} async-done(((bf16[1024,10]{1,0:T(8,128)(2,1)}), bf16[128,10]{1,0:T(8,128)(2,1)}) %reduce-scatter.39.cloned.1.call-update) | async-done | bytes 2576
  819.7 12.6 %all-reduce = (f32[1,2,128]{2,1,0:T(2,128)}, f32[1,10,128]{2,1,0:T(8,128)S(1)}) all-reduce(f32[1,2,128]{2,1,0:T(2,128)S(1)} %bitcast_convert_fusion.6, f32[1,10,128]{2,1,0:T(8,128)S(1)} %bitcast_convert_fusion.5), channel_id=1, replica_groups=mesh['dp'=8,'tensor'=4] {'tensor'}, use_global_device_ids=true, to_apply=%region_26.27 | all-reduce | flops 1536 | bytes 12288 | tf_op jit(solution)/shard_map/psum | solution.py:362
  (252 shorter events, 145.7 us)
Async XLA Ops:
  7.2 35.3 %all-gather.22.cloned.1.call-start = ((), (), s32[]{:S(2)}) async-start(), calls=%async_computation.19 | async-start | bytes 1769472 | tf_op jit(solution)/shard_map/all_gather | solution.py:315
  7.9 79.0 %all-gather.14.cloned.1.call-start = ((), (), s32[]{:S(2)}) async-start(), calls=%async_computation.10 | async-start | bytes 2621440 | tf_op jit(solution)/shard_map/all_gather | solution.py:156
  32.3 157.9 %reduce-scatter.21.cloned.1.call-start = ((), (), s32[]{:S(2)}) async-start(), calls=%async_computation.11 | async-start | bytes 5242880 | tf_op jit(solution)/shard_map/reduce_scatter | solution.py:172
  114.6 106.0 %all-gather.24.cloned.1.call-start = ((), (), s32[]{:S(2)}) async-start(), calls=%async_computation.20 | async-start | bytes 2359296 | tf_op jit(solution)/shard_map/all_gather | solution.py:317
  115.2 153.4 %all-gather.16.cloned.1.call-start = ((), (), s32[]{:S(2)}) async-start(), calls=%async_computation.12 | async-start | bytes 2621440 | tf_op jit(solution)/shard_map/all_gather | solution.py:181
  193.0 122.4 %all-gather.18.cloned.1.call-start = ((), (), s32[]{:S(2)}) async-start(), calls=%async_computation.14 | async-start | bytes 2621440 | tf_op jit(solution)/shard_map/all_gather | solution.py:228
  195.8 148.6 %all-gather.26.cloned.1.call-start = ((), (), s32[]{:S(2)}) async-start(), calls=%async_computation.21 | async-start | bytes 2359296 | tf_op jit(solution)/shard_map/all_gather | solution.py:318
  196.5 239.4 %reduce-scatter.25.cloned.1.call-start = ((), (), s32[]{:S(2)}) async-start(), calls=%async_computation.15 | async-start | bytes 5242880 | tf_op jit(solution)/shard_map/reduce_scatter | solution.py:238
  359.0 123.6 %reduce-scatter.23.cloned.1.call-start = ((), (), s32[]{:S(2)}) async-start(), calls=%async_computation.13 | async-start | bytes 2621440 | tf_op jit(solution)/shard_map/reduce_scatter | solution.py:189
  366.1 165.9 %all-gather.20.cloned.1.call-start = ((), (), s32[]{:S(2)}) async-start(), calls=%async_computation.16 | async-start | bytes 2621440 | tf_op jit(solution)/shard_map/all_gather | solution.py:252
  486.6 110.0 %reduce-scatter.35.cloned.1.call-start = ((), (), s32[]{:S(2)}) async-start(), calls=%async_computation.24 | async-start | bytes 2359296
  498.3 121.7 %reduce-scatter.29.cloned.1.call-start = ((), (), s32[]{:S(2)}) async-start(), calls=%async_computation.18 | async-start | bytes 2359296 | tf_op jit(solution)/shard_map/reduce_scatter | solution.py:345
  504.4 153.2 %reduce-scatter.33.cloned.1.call-start = ((), (), s32[]{:S(2)}) async-start(), calls=%async_computation.23 | async-start | bytes 589824
  537.3 162.0 %reduce-scatter.31.cloned.1.call-start = ((), (), s32[]{:S(2)}) async-start(), calls=%async_computation.22 | async-start | bytes 1769472
  591.5 153.7 %reduce-scatter.27.cloned.1.call-start = ((), (), s32[]{:S(2)}) async-start(), calls=%async_computation.17 | async-start | bytes 2621440 | tf_op jit(solution)/shard_map/reduce_scatter | solution.py:264
  596.2 149.1 %copy-start.1 = (bf16[256,1024]{1,0:T(8,128)(2,1)S(1)}, bf16[256,1024]{1,0:T(8,128)(2,1)}, u32[]{:S(2)}) copy-start(bf16[256,1024]{1,0:T(8,128)(2,1)} %param.13) | copy-start | bytes 1572868
  596.2 149.1 %copy-start.18 = (f32[1,1,1024]{2,1,0:T(1,128)S(1)}, f32[1,1,1024]{2,1,0:T(1,128)}, u32[]{:S(2)}) copy-start(f32[1,1,1024]{2,1,0:T(1,128)} %copy-done.17) | copy-start | bytes 12292
  596.2 149.1 %copy-start.20 = (f32[256]{0:T(256)S(1)}, f32[256]{0:T(256)}, u32[]{:S(2)}) copy-start(f32[256]{0:T(256)} %copy-done.19) | copy-start | bytes 3076
  596.2 150.5 %copy-start.24 = (f32[256]{0:T(256)S(1)}, f32[256]{0:T(256)}, u32[]{:S(2)}) copy-start(f32[256]{0:T(256)} %copy-done.23) | copy-start | bytes 3076
  596.2 150.5 %copy-start.22 = (f32[256]{0:T(256)S(1)}, f32[256]{0:T(256)}, u32[]{:S(2)}) copy-start(f32[256]{0:T(256)} %copy-done.21) | copy-start | bytes 3076
  596.2 186.2 %reduce-scatter.37.cloned.1.call-start = ((), (), s32[]{:S(2)}) async-start(), calls=%async_computation.25 | async-start | bytes 294912
  598.6 153.1 %copy-start.3 = (f32[256,1024]{1,0:T(8,128)S(1)}, f32[256,1024]{1,0:T(8,128)}, u32[]{:S(2)}) copy-start(f32[256,1024]{1,0:T(8,128)} %param.21) | copy-start | bytes 3145732
  598.6 153.1 %copy-start.5 = (f32[256,1024]{1,0:T(8,128)S(1)}, f32[256,1024]{1,0:T(8,128)}, u32[]{:S(2)}) copy-start(f32[256,1024]{1,0:T(8,128)} %copy-done.4) | copy-start | bytes 3145732
  749.3 69.6 %reduce-scatter.39.cloned.1.call-start = ((), (), s32[]{:S(2)}) async-start(), calls=%async_computation.26 | async-start | bytes 294912
  (26 other events, 358.9 us)
Sparse Core Ops, SparseCore 0:
  9.9 28.6 all-gather.21
  40.7 46.1 all-gather.13
  114.7 75.4 reduce-scatter.20
  192.1 28.3 all-gather.23
  222.6 45.9 all-gather.15
  270.7 44.6 all-gather.17
  317.4 26.8 all-gather.25
  359.1 76.7 reduce-scatter.24
  438.2 44.3 reduce-scatter.22
  486.7 45.2 all-gather.19
  535.7 39.9 reduce-scatter.34
  578.8 41.2 reduce-scatter.28
  623.4 34.1 reduce-scatter.32
  660.7 38.4 reduce-scatter.30
  701.4 43.8 reduce-scatter.26
  749.5 32.8 reduce-scatter.36
  785.3 33.5 reduce-scatter.38
where the time goes:
time: 848 us; the launch traced here: 840 us
  waiting for transfers between devices  610 us (72%)
  matrix products  91.4 us (11%)
  blocking collectives  41.5 us (5%)
  other arithmetic  38.9 us (5%)
  local copies, waits for them, and re-layouts  35.2 us (4%)
  between operations  14.7 us (2%)
    unnamed x22, waiting for transfers between devices  141 us
    reduce_scatter x1, waiting for transfers between devices, layer_forward(): lax.psum_scatter(attn_term(jnp.int32(0), local_rows * lax.axis_size('tens...  75 us
    reduce_scatter x1, waiting for transfers between devices, layer_backward(): lax.psum_scatter(lax.dot_general(hidden_grad, up_w, (((1,), (1,)), ((), (...  69.8 us
    all_gather x1, waiting for transfers between devices, layer_forward(): normed_two_kept = lax.all_gather(normed_two, 'tensor', axis=0, tiled=True)  48 us
    reduce_scatter x1, waiting for transfers between devices, layer_forward(): lax.psum_scatter(jnp.dot(active, down_w, preferred_element_type=jnp.float...  45.1 us
    all_gather x1, waiting for transfers between devices, layer_forward(): normed_full = lax.all_gather(normed, 'tensor', axis=0, tiled=True)  44.5 us
    reduce_scatter x1, waiting for transfers between devices, layer_backward(): lax.psum_scatter(attn_term(jnp.int32(0), local_rows * lax.axis_size('tens...  43.8 us
    all_gather x1, waiting for transfers between devices, layer_backward(): lax.all_gather(branch_grad, 'tensor', axis=0, tiled=True)  40.3 us
  transfers between devices with their start and end apart: 17, of which 15 were waited for; matrix products, arithmetic and copies ran while one was open for 14% of the time, Pallas kernels for 0%

commit v1 on v0

--- a/solution.py
+++ b/solution.py
@@ -178,7 +178,14 @@
         + bias_rows[3]
     )
     normed_two = layer_norm(middle, gain_rows[1], bias_rows[4]).astype(jnp.bfloat16)
-    normed_two_kept = lax.all_gather(normed_two, "tensor", axis=0, tiled=True)
+    ring = [normed_two]
+    for hop in range(3):
+        ring.append(lax.ppermute(ring[-1], "tensor", [(dev, (dev + 1) % 4) for dev in range(4)]))
+    normed_two_kept = jnp.roll(
+        jnp.concatenate(ring[::-1], axis=0),
+        (lax.axis_index("tensor") + 1) * ring[0].shape[0],
+        axis=0,
+    )
     unit_width = up_w.shape[1]
     up_bias = lax.dynamic_slice_in_dim(
         bias_rows[6:10].reshape(-1), tensor_rank * unit_width, unit_width, 0

time: 848 us -> 804 us (0.948)
  waiting for transfers between devices: 610 us -> 555 us
  local copies, waits for them, and re-layouts: 35.2 us -> 44 us
    all_gather x1 -> x0, waiting for transfers between devices: 48 us -> none  [layer_forward(): normed_two_kept = lax.all_gather(normed_two, 'tensor', axis=0, tiled=True)]
    ppermute x0 -> x3, waiting for transfers between devices: none -> 45.8 us  [layer_forward(): lax.ppermute(ring[-1], 'tensor', [(dev, (dev + 1) % 4) for dev in range(4)])]
    all_gather x1, waiting for transfers between devices: 40.3 us -> 13.4 us  [layer_backward(): lax.all_gather(branch_grad, 'tensor', axis=0, tiled=True)]
    all_gather x1, waiting for transfers between devices: 23.8 us -> 0.01 us  [per_device(): lax.all_gather(up_weight[layer_index], 'dp', axis=0, tiled=True)]
    unnamed x66 -> x78, local copies, waits for them, and re-layouts: 23.7 us -> 32.7 us
    unnamed x22 -> x21, waiting for transfers between devices: 141 us -> 141 us
  transfers between devices with their start and end apart: 17 -> 19, of which waited for: 15 -> 16; matrix products, arithmetic and copies ran while one was open for 14% -> 15% of each run, Pallas kernels for 0% -> 0%
where the time goes in v1:
time: 804 us; the launch traced here: 795 us
  waiting for transfers between devices  555 us (69%)
  matrix products  91.9 us (11%)
  local copies, waits for them, and re-layouts  44 us (5%)
  blocking collectives  41 us (5%)
  other arithmetic  39.1 us (5%)
  between operations  14.7 us (2%)
    unnamed x21, waiting for transfers between devices  141 us
    reduce_scatter x1, waiting for transfers between devices, layer_forward(): lax.psum_scatter(attn_term(jnp.int32(0), local_rows * lax.axis_size('tens...  72.4 us
    reduce_scatter x1, waiting for transfers between devices, layer_backward(): lax.psum_scatter(lax.dot_general(hidden_grad, up_w, (((1,), (1,)), ((), (...  69.6 us
    ppermute x3, waiting for transfers between devices, layer_forward(): lax.ppermute(ring[-1], 'tensor', [(dev, (dev + 1) % 4) for dev in range(4)])  45.8 us
    reduce_scatter x1, waiting for transfers between devices, layer_forward(): lax.psum_scatter(jnp.dot(active, down_w, preferred_element_type=jnp.float...  45.1 us
    all_gather x1, waiting for transfers between devices, layer_forward(): normed_full = lax.all_gather(normed, 'tensor', axis=0, tiled=True)  44.1 us
    reduce_scatter x1, waiting for transfers between devices, layer_backward(): lax.psum_scatter(attn_term(jnp.int32(0), local_rows * lax.axis_size('tens...  43.8 us
    unnamed x78, local copies, waits for them, and re-layouts  32.7 us
  transfers between devices with their start and end apart: 19, of which 16 were waited for; matrix products, arithmetic and copies ran while one was open for 15% of the time, Pallas kernels for 0%

profile of v1, /device:TPU:0, one launch (start us, length us, event | category | flops | bytes accessed | tf_op | source)
XLA Modules:
  0.0 795.2 jit_solution(6347811315085008636)
XLA Ops:
  7.9 10.3 %all-gather = bf16[1,2,1024]{2,1,0:T(2,128)(2,1)S(1)} all-gather(bf16[1,2,128]{2,1,0:T(2,128)(2,1)} %param.19), channel_id=2, replica_groups=mesh['dp'=8,'tensor'=4] {'dp'}, dimensions={2}, use_global_device_ids=true | all-gather | bytes 4608 | tf_op jit(solution)/shard_map/all_gather | solution.py:326
  18.3 8.7 %all-gather.1 = bf16[1,10,1024]{2,1,0:T(8,128)(2,1)S(1)} all-gather(bf16[1,10,128]{2,1,0:T(8,128)(2,1)} %param.20), channel_id=3, replica_groups=mesh['dp'=8,'tensor'=4] {'dp'}, dimensions={2}, use_global_device_ids=true | all-gather | bytes 23040 | tf_op jit(solution)/shard_map/all_gather | solution.py:327
  33.0 9.3 %all-gather.3 = bf16[1,256,1024]{2,1,0:T(8,128)(2,1)S(1)} all-gather(bf16[1,256,128]{2,1,0:T(8,128)(2,1)} %param.16), channel_id=5, replica_groups=mesh['dp'=8,'tensor'=4] {'dp'}, dimensions={2}, use_global_device_ids=true | all-gather | bytes 589824 | tf_op jit(solution)/shard_map/all_gather | solution.py:323
  42.4 44.1 %all-gather.13.cloned.1.call-done = bf16[1024,1024]{1,0:T(8,128)(2,1)} async-done(((bf16[256,1024]{1,0:T(8,128)(2,1)}), bf16[1024,1024]{1,0:T(8,128)(2,1)}) %all-gather.13.cloned.1.call-update) | async-done | bytes 2097168 | tf_op jit(solution)/shard_map/all_gather | solution.py:156
  93.3 18.3 %while.43 = (s32[]{:T(128)}, bf16[2,512,256]{2,1,0:T(8,128)(2,1)S(1)}, f32[2,4,512]{2,1,0:T(4,128)S(1)}, s32[2]{0:T(128)S(1)}, s32[1024]{0:T(1024)S(1)}, /*index...) while((s32[]{:T(128)}, ...), condition=%wide.region_5.6_spmd, body=%wide.region_2.5_spmd.sunk | while | flops 563740160 | bytes 32594288 | solution.py:66
  118.3 72.4 %reduce-scatter.21.cloned.1.call-done = f32[256,1024]{1,0:T(8,128)} async-done(((f32[1024,1024]{1,0:T(8,128)}), f32[256,1024]{1,0:T(8,128)}) %reduce-scatter.21.cloned.1.call-update) | async-done | bytes 1048592 | tf_op jit(solution)/shard_map/reduce_scatter | solution.py:172
  194.2 14.0 %collective-permute-done = bf16[256,1024]{1,0:T(8,128)(2,1)S(1)} collective-permute-done((bf16[256,1024]{1,0:T(8,128)(2,1)S(1)}, bf16[256,1024]{1,0:T(8,128)(2,1)S(1)}, u32[]{:S(2)}, u32[]{:S(2)}) %collective-permute-start) | collective-permute-done | bytes 524320 | tf_op jit(solution)/shard_map/ppermute | solution.py:183
  208.2 14.7 %collective-permute-done.1 = bf16[256,1024]{1,0:T(8,128)(2,1)} collective-permute-done((bf16[256,1024]{1,0:T(8,128)(2,1)S(1)}, bf16[256,1024]{1,0:T(8,128)(2,1)}, u32[]{:S(2)}, u32[]{:S(2)}) %collective-permute-start.1) | collective-permute-done | bytes 524320 | tf_op jit(solution)/shard_map/ppermute | solution.py:183
  223.2 17.1 %collective-permute-done.2 = bf16[256,1024]{1,0:T(8,128)(2,1)} collective-permute-done((bf16[256,1024]{1,0:T(8,128)(2,1)}, bf16[256,1024]{1,0:T(8,128)(2,1)}, u32[]{:S(2)}, u32[]{:S(2)}) %collective-permute-start.2) | collective-permute-done | bytes 524320 | tf_op jit(solution)/shard_map/ppermute | solution.py:183
  258.1 13.4 %all-gather.15.cloned.1.call-done = bf16[1024,1024]{1,0:T(8,128)(2,1)} async-done(((bf16[256,1024]{1,0:T(8,128)(2,1)}), bf16[1024,1024]{1,0:T(8,128)(2,1)}) %all-gather.15.cloned.1.call-update) | async-done | bytes 2097168 | tf_op jit(solution)/shard_map/all_gather | solution.py:235
  271.5 28.4 %all-gather.23.cloned.1.call-done = bf16[1,1024,1024]{2,1,0:T(8,128)(2,1)} async-done(((bf16[1,1024,128]{2,1,0:T(8,128)(2,1)}), bf16[1,1024,1024]{2,1,0:T(8,128)(2,1)}) %all-gather.23.cloned.1.call-update) | async-done | bytes 2097168 | tf_op jit(solution)/shard_map/all_gather | solution.py:325
  299.9 9.0 %convert_reduce_fusion = (bf16[1024]{0:T(1024)(128)(2,1)}, bf16[1024,1024]{1,0:T(8,128)(2,1)S(1)}) fusion(f32[1024,1024]{1,0:T(8,128)} %fusion.37, f32[1024]{0:T(1024)S(1)} %dynamic_slice.73, bf16[1024,1024]{1,0:T(8,128)(2,1)} %all-gather.15.cloned.1.call-done, bf16[1,1024,1024]{2,1,0:T(8,128)(2,1)} %all-gather.23.cloned.1.call-done), kind=kOutput, calls=%fused_computation.47 | convolution fusion | flops 2171599872 | bytes 10491904 | tf_op jit(solution)/shard_map/dot_general | solution.py:141
  321.9 69.6 %reduce-scatter.25.cloned.1.call-done = f32[256,1024]{1,0:T(8,128)} async-done(((f32[1024,1024]{1,0:T(8,128)}), f32[256,1024]{1,0:T(8,128)}) %reduce-scatter.25.cloned.1.call-update) | async-done | bytes 1048592 | tf_op jit(solution)/shard_map/reduce_scatter | solution.py:245
  393.1 45.1 %reduce-scatter.23.cloned.1.call-done = bf16[256,1024]{1,0:T(8,128)(2,1)} async-done(((bf16[1024,1024]{1,0:T(8,128)(2,1)}), bf16[256,1024]{1,0:T(8,128)(2,1)}) %reduce-scatter.23.cloned.1.call-update) | async-done | bytes 524304 | tf_op jit(solution)/shard_map/reduce_scatter | solution.py:196
  442.2 7.2 convolution_convert_fusion
  459.6 28.0 %all-gather.17.cloned.1.call-done = bf16[1024,1024]{1,0:T(8,128)(2,1)} async-done(((bf16[256,1024]{1,0:T(8,128)(2,1)}), bf16[1024,1024]{1,0:T(8,128)(2,1)}) %all-gather.17.cloned.1.call-update) | async-done | bytes 2097168 | tf_op jit(solution)/shard_map/all_gather | solution.py:259
  496.4 33.4 %while.44 = (s32[]{:T(128)}, f32[1024,4,64]{0,2,1:T(8,128)S(1)}, f32[1024,4,64]{0,2,1:T(8,128)}, bf16[2,512,4,64]{1,3,2,0:T(8,128)(2,1)}, s32[2]{0:T(128)S(1)}, ...) while((s32[]{:T(128)}, f32[1024,4,64]{0,2,1:T(8,128)S(1)}, ...), condition=%wide.region_15.16_spmd.clone, body=%wide.region_13.15_spmd.clone.sunk | while | flops 1376648704 | bytes 88685112 | solution.py:119
  552.5 23.1 %reduce-scatter.29.cloned.1.call-done = bf16[128,1024]{1,0:T(8,128)(2,1)} async-done(((bf16[1024,1024]{1,0:T(8,128)(2,1)}), bf16[128,1024]{1,0:T(8,128)(2,1)}) %reduce-scatter.29.cloned.1.call-update) | async-done | bytes 262160 | tf_op jit(solution)/shard_map/reduce_scatter | solution.py:352
  578.8 34.2 %reduce-scatter.33.cloned.1.call-done = bf16[128,256]{1,0:T(8,128)(2,1)} async-done(((bf16[1024,256]{1,0:T(8,128)(2,1)}), bf16[128,256]{1,0:T(8,128)(2,1)}) %reduce-scatter.33.cloned.1.call-update) | async-done | bytes 65552
  614.6 40.2 %reduce-scatter.31.cloned.1.call-done = bf16[128,768]{1,0:T(8,128)(2,1)} async-done(((bf16[1024,768]{1,0:T(8,128)(2,1)}), bf16[128,768]{1,0:T(8,128)(2,1)}) %reduce-scatter.31.cloned.1.call-update) | async-done | bytes 196624
  657.0 43.8 %reduce-scatter.27.cloned.1.call-done = bf16[256,1024]{1,0:T(8,128)(2,1)} async-done(((bf16[1024,1024]{1,0:T(8,128)(2,1)}), bf16[256,1024]{1,0:T(8,128)(2,1)}) %reduce-scatter.27.cloned.1.call-update) | async-done | bytes 524304 | tf_op jit(solution)/shard_map/reduce_scatter | solution.py:271
  708.6 29.3 %reduce-scatter.37.cloned.1.call-done = bf16[128,2]{1,0:T(8,128)(2,1)} async-done(((bf16[1024,2]{1,0:T(8,128)(2,1)}), bf16[128,2]{1,0:T(8,128)(2,1)}) %reduce-scatter.37.cloned.1.call-update) | async-done | bytes 528
  738.7 35.7 %reduce-scatter.39.cloned.1.call-done = bf16[128,10]{1,0:T(8,128)(2,1)} async-done(((bf16[1024,10]{1,0:T(8,128)(2,1)}), bf16[128,10]{1,0:T(8,128)(2,1)}) %reduce-scatter.39.cloned.1.call-update) | async-done | bytes 2576
  775.2 12.6 %all-reduce = (f32[1,2,128]{2,1,0:T(2,128)}, f32[1,10,128]{2,1,0:T(8,128)S(1)}) all-reduce(f32[1,2,128]{2,1,0:T(2,128)S(1)} %bitcast_convert_fusion.6, f32[1,10,128]{2,1,0:T(8,128)S(1)} %bitcast_convert_fusion.5), channel_id=1, replica_groups=mesh['dp'=8,'tensor'=4] {'tensor'}, use_global_device_ids=true, to_apply=%region_26.27 | all-reduce | flops 1536 | bytes 12288 | tf_op jit(solution)/shard_map/psum | solution.py:369
  (269 shorter events, 163.7 us)
Async XLA Ops:
  7.2 35.2 %all-gather.19.cloned.1.call-start = ((), (), s32[]{:S(2)}) async-start(), calls=%async_computation.18 | async-start | bytes 1769472 | tf_op jit(solution)/shard_map/all_gather | solution.py:322
  7.9 78.6 %all-gather.13.cloned.1.call-start = ((), (), s32[]{:S(2)}) async-start(), calls=%async_computation.10 | async-start | bytes 2621440 | tf_op jit(solution)/shard_map/all_gather | solution.py:156
  32.9 157.8 %reduce-scatter.21.cloned.1.call-start = ((), (), s32[]{:S(2)}) async-start(), calls=%async_computation.11 | async-start | bytes 5242880 | tf_op jit(solution)/shard_map/reduce_scatter | solution.py:172
  115.0 136.6 %all-gather.21.cloned.1.call-start = ((), (), s32[]{:S(2)}) async-start(), calls=%async_computation.19 | async-start | bytes 2359296 | tf_op jit(solution)/shard_map/all_gather | solution.py:324
  115.6 155.9 %all-gather.15.cloned.1.call-start = ((), (), s32[]{:S(2)}) async-start(), calls=%async_computation.13 | async-start | bytes 2621440 | tf_op jit(solution)/shard_map/all_gather | solution.py:235
  117.7 182.3 %all-gather.23.cloned.1.call-start = ((), (), s32[]{:S(2)}) async-start(), calls=%async_computation.20 | async-start | bytes 2359296 | tf_op jit(solution)/shard_map/all_gather | solution.py:325
  118.2 273.2 %reduce-scatter.25.cloned.1.call-start = ((), (), s32[]{:S(2)}) async-start(), calls=%async_computation.14 | async-start | bytes 5242880 | tf_op jit(solution)/shard_map/reduce_scatter | solution.py:245
  192.6 15.5 %collective-permute-start = (bf16[256,1024]{1,0:T(8,128)(2,1)S(1)}, bf16[256,1024]{1,0:T(8,128)(2,1)S(1)}, u32[]{:S(2)}, u32[]{:S(2)}) collective-permute-start(bf16[256,1024]{1,0:T(8,128)(2,1)S(1)} %add_convert_fusion.1), channel_id=1, source_target_pairs={{0,1},{1,2},{2,3},{3,0},{4,5},{5,6},{6,7},{7,4},{8,9},{9,10},{10,1... | collective-permute-start | bytes 1572872 | tf_op jit(solution)/shard_map/ppermute | solution.py:183
  208.2 14.7 %collective-permute-start.1 = (bf16[256,1024]{1,0:T(8,128)(2,1)S(1)}, bf16[256,1024]{1,0:T(8,128)(2,1)}, u32[]{:S(2)}, u32[]{:S(2)}) collective-permute-start(bf16[256,1024]{1,0:T(8,128)(2,1)S(1)} %collective-permute-done), channel_id=1, source_target_pairs={{0,1},{1,2},{2,3},{3,0},{4,5},{5,6},{6,7},{7,4},{8,9},{9,10},{10,1... | collective-permute-start | bytes 1572872 | tf_op jit(solution)/shard_map/ppermute | solution.py:183
  222.9 17.4 %collective-permute-start.2 = (bf16[256,1024]{1,0:T(8,128)(2,1)}, bf16[256,1024]{1,0:T(8,128)(2,1)}, u32[]{:S(2)}, u32[]{:S(2)}) collective-permute-start(bf16[256,1024]{1,0:T(8,128)(2,1)} %collective-permute-done.1), channel_id=1, source_target_pairs={{0,1},{1,2},{2,3},{3,0},{4,5},{5,6},{6,7},{7,4},{8,9},{9,10},{10,1... | collective-permute-start | bytes 1572872 | tf_op jit(solution)/shard_map/ppermute | solution.py:183
  314.6 123.6 %reduce-scatter.23.cloned.1.call-start = ((), (), s32[]{:S(2)}) async-start(), calls=%async_computation.12 | async-start | bytes 2621440 | tf_op jit(solution)/shard_map/reduce_scatter | solution.py:196
  321.6 165.9 %all-gather.17.cloned.1.call-start = ((), (), s32[]{:S(2)}) async-start(), calls=%async_computation.15 | async-start | bytes 2621440 | tf_op jit(solution)/shard_map/all_gather | solution.py:259
  442.1 108.3 %reduce-scatter.35.cloned.1.call-start = ((), (), s32[]{:S(2)}) async-start(), calls=%async_computation.23 | async-start | bytes 2359296
  453.5 122.1 %reduce-scatter.29.cloned.1.call-start = ((), (), s32[]{:S(2)}) async-start(), calls=%async_computation.17 | async-start | bytes 2359296 | tf_op jit(solution)/shard_map/reduce_scatter | solution.py:352
  459.5 153.5 %reduce-scatter.33.cloned.1.call-start = ((), (), s32[]{:S(2)}) async-start(), calls=%async_computation.22 | async-start | bytes 589824
  492.7 162.0 %reduce-scatter.31.cloned.1.call-start = ((), (), s32[]{:S(2)}) async-start(), calls=%async_computation.21 | async-start | bytes 1769472
  545.0 155.8 %reduce-scatter.27.cloned.1.call-start = ((), (), s32[]{:S(2)}) async-start(), calls=%async_computation.16 | async-start | bytes 2621440 | tf_op jit(solution)/shard_map/reduce_scatter | solution.py:271
  550.1 150.7 %copy-start.23 = (f32[256]{0:T(256)S(1)}, f32[256]{0:T(256)}, u32[]{:S(2)}) copy-start(f32[256]{0:T(256)} %copy-done.22) | copy-start | bytes 3076
  550.1 152.2 %copy-start.27 = (f32[256]{0:T(256)S(1)}, f32[256]{0:T(256)}, u32[]{:S(2)}) copy-start(f32[256]{0:T(256)} %copy-done.26) | copy-start | bytes 3076
  550.1 152.2 %copy-start.25 = (f32[256]{0:T(256)S(1)}, f32[256]{0:T(256)}, u32[]{:S(2)}) copy-start(f32[256]{0:T(256)} %copy-done.24) | copy-start | bytes 3076
  550.1 187.8 %reduce-scatter.37.cloned.1.call-start = ((), (), s32[]{:S(2)}) async-start(), calls=%async_computation.24 | async-start | bytes 294912
  552.4 154.7 %copy-start.4 = (f32[256,1024]{1,0:T(8,128)S(1)}, f32[256,1024]{1,0:T(8,128)}, u32[]{:S(2)}) copy-start(f32[256,1024]{1,0:T(8,128)} %param.21) | copy-start | bytes 3145732
  552.4 154.7 %copy-start.6 = (f32[256,1024]{1,0:T(8,128)S(1)}, f32[256,1024]{1,0:T(8,128)}, u32[]{:S(2)}) copy-start(f32[256,1024]{1,0:T(8,128)} %copy-done.5) | copy-start | bytes 3145732
  704.9 69.6 %reduce-scatter.39.cloned.1.call-start = ((), (), s32[]{:S(2)}) async-start(), calls=%async_computation.25 | async-start | bytes 294912
  (31 other events, 718.4 us)
Sparse Core Ops, SparseCore 0:
  9.9 28.4 all-gather.18
  40.6 45.9 all-gather.12
  115.1 75.4 reduce-scatter.20
  192.6 28.3 all-gather.20
  223.0 48.4 all-gather.14
  273.4 26.4 all-gather.22
  314.7 76.7 reduce-scatter.24
  393.8 44.3 reduce-scatter.22
  442.3 45.2 all-gather.16
  491.0 39.9 reduce-scatter.34
  534.3 41.2 reduce-scatter.28
  578.8 34.1 reduce-scatter.32
  616.3 38.4 reduce-scatter.30
  656.9 43.8 reduce-scatter.26
  705.0 32.8 reduce-scatter.36
  740.8 33.5 reduce-scatter.38
